TPU v7x, 512 devices: a whole 4x4x16 slice. The times are simulated.
512 devices in a mesh: slab: 32 (over y, z_hi, x), shots: 16 (over z_lo, core).
Axes of the slice: x: 4, y: 4, z: 16 (z_hi: 2, z_lo: 8; z = z_hi * 8 + z_lo), core: 2. Of those that a mesh axis runs over, the one named last changes fastest.
Arguments:
- src_prev: float32 [32, 256, 64, 128], P('shots', 'slab'), may hold values from -6 to 6
- src_cur: float32 [32, 256, 64, 128], P('shots', 'slab'), may hold values from -6 to 6
- rcv_prev: float32 [32, 256, 64, 128], P('shots', 'slab'), may hold values from -6 to 6
- rcv_cur: float32 [32, 256, 64, 128], P('shots', 'slab'), may hold values from -6 to 6
- velocity: float32 [256, 64, 128], P('slab'), may hold values from 0.05 to 0.18
- wavelet: float32 [2, 32], P(None, 'shots'), may hold values from -6 to 6
- residual_traces: float32 [2, 32, 256], P(None, 'shots'), may hold values from -6 to 6
- source_depth: int32 [32], P('shots'), may hold values from 0 to 255
- source_y: int32 [32], P('shots'), may hold values from 21 to 42
- source_x: int32 [32], P('shots'), may hold values from 42 to 85
- half_y: int32 [32], P('shots'), may hold values from 10 to 21
- half_x: int32 [32], P('shots'), may hold values from 21 to 42
- receiver_cell: int32 [32, 256], P('shots'), may hold values from 0 to 2097151
Outputs:
- src_last: float32 [32, 256, 64, 128], P('shots', 'slab')
- rcv_last: float32 [32, 256, 64, 128], P('shots', 'slab')
- image: float32 [256, 64, 128], P('slab')
All inputs are finite; a program needn't handle non-finite values.
Results may differ from a plain program's by a relative error of at most 0.0003.
Values sent between devices are 32-bit elements; how exact they have to be, the bound alone decides.
A program may use at most 64 MiB of HBM per device.

v0:
```python
import jax
import jax.numpy as jnp
from jax import lax
from jax.sharding import PartitionSpec as P

STEPS = 2
COEF = (-205.0 / 72.0, 8.0 / 5.0, -1.0 / 5.0, 8.0 / 315.0, -1.0 / 560.0)


def extended(block, sides, width):
    for axis, dim in sides:
        count = lax.axis_size(axis)
        forward = [(i, i + 1) for i in range(count - 1)]
        backward = [(target, source) for source, target in forward]
        low = lax.ppermute(
            lax.slice_in_dim(block, block.shape[dim] - width, None, axis=dim), axis, forward
        )
        high = lax.ppermute(lax.slice_in_dim(block, 0, width, axis=dim), axis, backward)
        block = jnp.concatenate([low, block, high], axis=dim)
    return block


def laplace(padded):
    axis_z = padded.ndim - 3
    length = padded.shape[axis_z] - 8
    center = lax.slice_in_dim(padded, 4, 4 + length, axis=axis_z)
    total = 3.0 * COEF[0] * center
    for shift_k in range(1, 5):
        upper = lax.slice_in_dim(padded, 4 + shift_k, 4 + shift_k + length, axis=axis_z)
        lower = lax.slice_in_dim(padded, 4 - shift_k, 4 - shift_k + length, axis=axis_z)
        total = total + COEF[shift_k] * (upper + lower)
    widths = [(0, 0)] * (center.ndim - 2) + [(4, 4), (4, 4)]
    plane = jnp.pad(center, widths)
    rows_y = center.shape[-2]
    cols_x = center.shape[-1]
    for shift_k in range(1, 5):
        side_y = (
            plane[..., 4 + shift_k : 4 + shift_k + rows_y, 4 : 4 + cols_x]
            + plane[..., 4 - shift_k : 4 - shift_k + rows_y, 4 : 4 + cols_x]
        )
        side_x = (
            plane[..., 4 : 4 + rows_y, 4 + shift_k : 4 + shift_k + cols_x]
            + plane[..., 4 : 4 + rows_y, 4 - shift_k : 4 - shift_k + cols_x]
        )
        total = total + COEF[shift_k] * (side_y + side_x)
    return total


def band_mask(source_y, source_x, half_y, half_x, rows_y, cols_x):
    grid_y = jnp.arange(rows_y, dtype=jnp.int32)
    grid_x = jnp.arange(cols_x, dtype=jnp.int32)
    inside_y = jnp.abs(grid_y[None, :, None] - source_y[:, None, None]) <= half_y[:, None, None]
    inside_x = jnp.abs(grid_x[None, None, :] - source_x[:, None, None]) <= half_x[:, None, None]
    return (inside_y & inside_x).astype(jnp.float32)


def inject(cells, values, begin, length, rows_y, cols_x):
    plane = rows_y * cols_x
    depth = cells // plane
    rest = cells - depth * plane
    local = depth - begin
    valid = (local >= 0) & (local < length)
    flat = jnp.where(valid, local * plane + rest, 0)
    amounts = jnp.where(valid, values, jnp.zeros_like(values))
    count = cells.shape[0]
    rows = jnp.broadcast_to(jnp.arange(count, dtype=jnp.int32)[:, None], flat.shape)
    field = jnp.zeros((count, length * plane), jnp.float32).at[rows, flat].add(amounts)
    return field.reshape(count, length, rows_y, cols_x)


def per_device(
    src_prev,
    src_cur,
    rcv_prev,
    rcv_cur,
    velocity,
    wavelet,
    residual_traces,
    source_depth,
    source_y,
    source_x,
    half_y,
    half_x,
    receiver_cell,
):
    shot_count, depth, rows_y, cols_x = src_cur.shape
    start = lax.axis_index("slab") * depth
    mask = band_mask(source_y, source_x, half_y, half_x, rows_y, cols_x)[:, None]
    scells = (source_depth * rows_y * cols_x + source_y * cols_x + source_x)[:, None]
    terms = []
    up, u, vp, v = (src_prev, src_cur, rcv_prev, rcv_cur)
    for step in range(STEPS):
        stacked = jnp.stack([u, v])
        padded = extended(stacked, (("slab", 2),), 4)
        lap = laplace(padded)
        sdelta = inject(scells, wavelet[step][:, None], start, depth, rows_y, cols_x)
        rdelta = inject(receiver_cell, residual_traces[step], start, depth, rows_y, cols_x)
        sdelta, rdelta = (sdelta, rdelta)
        unew = mask * (2.0 * u - up + velocity * lap[0] + sdelta)
        vnew = mask * (2.0 * v - vp + velocity * lap[1] + rdelta)
        terms.append(jnp.sum((unew - 2.0 * u + up) * vnew, axis=0))
        up, u, vp, v = (u, unew, v, vnew)
    src_last, rcv_last = (u, v)
    local_sum = terms[0]
    for extra in terms[1:]:
        local_sum = local_sum + extra
    image = lax.psum(local_sum, "shots")
    return (src_last, rcv_last, image)


def solution(mesh):
    return jax.shard_map(
        per_device,
        mesh=mesh,
        in_specs=(
            P("shots", "slab", None, None),
            P("shots", "slab", None, None),
            P("shots", "slab", None, None),
            P("shots", "slab", None, None),
            P("slab", None, None),
            P(None, "shots"),
            P(None, "shots", None),
            P("shots"),
            P("shots"),
            P("shots"),
            P("shots"),
            P("shots"),
            P("shots", None),
        ),
        out_specs=(
            P("shots", "slab", None, None),
            P("shots", "slab", None, None),
            P("slab", None, None),
        ),
        check_vma=False,
    )
```

profile of v0, /device:TPU:1, one launch (start us, length us, event | category | flops | bytes accessed | tf_op | source)
XLA Modules:
  0.0 348.8 jit_solution(7300250642595813293)
XLA Ops:
  7.2 0.0 copy-start.7
  7.2 0.0 copy-start.6
  7.2 0.0 copy-start.8
  7.2 0.0 copy-start.9
  7.2 0.0 copy-start.11
  7.2 0.0 copy-start.10
  7.2 0.0 all-reduce.4.cloned.1.call-start
  7.3 2.3 fusion.58
  9.5 1.3 collective-permute-start
  10.8 4.6 %collective-permute-start.1 = (f32[2,2,4,64,128]{4,3,2,1,0:T(8,128)}, f32[2,2,4,64,128]{4,3,2,1,0:T(8,128)S(1)}, u32[]{:S(2)}, u32[]{:S(2)}) collective-permute-start(f32[2,2,4,64,128]{4,3,2,1,0:T(8,128)} %get-tuple-element.21), channel_id=1, source_target_pairs={{0,16},{16,32},{32,48},{48,64},{64,80},{80,96},{96,112},{112,128},... | collective-permute-start | bytes 1572872 | tf_op jit(solution)/shard_map/ppermute | solution.py:15
  15.5 0.0 copy-done.7
  15.5 0.0 copy-done.6
  15.5 0.0 copy-done.8
  15.5 0.0 copy-done.9
  15.5 0.0 copy-done.11
  15.6 0.0 copy-done.10
  15.6 0.1 copy.17
  15.7 0.2 fusion.83
  15.9 0.1 broadcast.180.clone.1
  16.1 0.6 scatter_fusion
  16.8 0.1 broadcast.180.clone
  16.9 0.0 copy-start.12
  16.9 0.0 copy-start
  16.9 0.0 copy-start.1
  16.9 24.8 %scatter_fusion.1 = f32[2,65536]{1,0:T(2,128)S(1)} fusion(f32[2,65536]{1,0:T(2,128)S(1)} %broadcast.180.clone, s32[512]{0:T(512)S(1)} %bitcast.87, f32[512]{0:T(512)S(1)} %bitcast.111), kind=kCustom, calls=%fused_computation.1 | custom fusion | flops 512 | bytes 10240 | tf_op jit(solution)/shard_map/scatter-add | solution.py:67
  41.7 0.0 copy-start.13
  41.8 0.0 copy-done.12
  41.8 0.1 abs_compare_fusion
  41.9 0.0 copy-done
  41.9 0.0 copy-done.1
  41.9 0.1 pad_maximum_fusion.2
  42.0 0.4 copy-done.13
  42.4 0.1 abs_compare_fusion.1
  42.5 0.1 and_convert_fusion
  42.6 0.0 collective-permute-done
  42.6 0.0 collective-permute-done.1
  42.6 0.4 pad_maximum_fusion
  43.0 0.0 copy-start.2
  43.0 0.0 copy-start.4
  43.0 0.0 copy-start.5
  43.0 2.5 fusion.6
  45.5 0.0 copy-done.2
  45.5 0.0 copy-done.4
  45.5 0.0 copy-done.5
  45.5 0.5 fusion.71
  46.0 1.0 fusion.56
  47.0 1.3 collective-permute-start.2
  48.3 4.8 %collective-permute-start.3 = (f32[2,2,4,64,128]{4,3,2,1,0:T(8,128)}, f32[2,2,4,64,128]{4,3,2,1,0:T(8,128)}, u32[]{:S(2)}, u32[]{:S(2)}) collective-permute-start(f32[2,2,4,64,128]{4,3,2,1,0:T(8,128)} %get-tuple-element.17), channel_id=1, source_target_pairs={{0,16},{16,32},{32,48},{48,64},{64,80},{80,96},{96,112},{112,128},... | collective-permute-start | bytes 1572872 | tf_op jit(solution)/shard_map/ppermute | solution.py:15
  53.1 0.1 broadcast.180.clone.3
  53.3 0.6 scatter_fusion.2
  54.0 0.1 broadcast.180.clone.2
  54.1 24.8 %scatter_fusion.3 = f32[2,65536]{1,0:T(2,128)S(1)} fusion(f32[2,65536]{1,0:T(2,128)S(1)} %broadcast.180.clone.2, s32[512]{0:T(512)S(1)} %bitcast.88, f32[512]{0:T(512)S(1)} %bitcast.110), kind=kCustom, calls=%fused_computation.3 | custom fusion | flops 512 | bytes 10240 | tf_op jit(solution)/shard_map/scatter-add | solution.py:67
  78.9 0.1 pad_maximum_fusion.3
  79.0 0.0 collective-permute-done.2
  79.0 0.0 collective-permute-done.3
  79.0 1.6 pad_maximum_fusion.1
  80.7 0.0 copy-start.3
  80.7 2.5 fusion.26
  83.1 0.0 copy-done.3
  83.1 1.6 multiply_reduce_fusion
  84.8 0.7 add.287
  85.5 0.0 all-reduce.4.cloned.1.call-update
  85.5 254.8 %all-reduce.4.cloned.1.call-done = f32[8,64,128]{2,1,0:T(8,128)} async-done(((f32[8,64,128]{2,1,0:T(8,128)}), f32[8,64,128]{2,1,0:T(8,128)}) %all-reduce.4.cloned.1.call-update) | async-done | bytes 262160 | tf_op jit(solution)/shard_map/psum | solution.py:107
  340.3 1.7 copy.30
  (15 shorter events, 0.2 us)
Async XLA Ops:
  7.2 8.3 %copy-start.7 = (f32[2,2,256]{2,1,0:T(2,128)S(1)}, f32[2,2,256]{2,1,0:T(2,128)}, u32[]{:S(2)}) copy-start(f32[2,2,256]{2,1,0:T(2,128)} %param.19) | copy-start | bytes 12292
  7.2 8.3 %copy-start.6 = (s32[2,256]{1,0:T(2,128)S(1)}, s32[2,256]{1,0:T(2,128)}, u32[]{:S(2)}) copy-start(s32[2,256]{1,0:T(2,128)} %param.25) | copy-start | bytes 6148
  7.2 8.3 %copy-start.8 = (f32[2,2]{1,0:T(2,128)S(1)}, f32[2,2]{1,0:T(2,128)}, u32[]{:S(2)}) copy-start(f32[2,2]{1,0:T(2,128)} %param.18) | copy-start | bytes 52
  7.2 8.3 %copy-start.9 = (s32[2]{0:T(128)S(1)}, s32[2]{0:T(128)}, u32[]{:S(2)}) copy-start(s32[2]{0:T(128)} %param.20) | copy-start | bytes 28
  7.2 8.3 %copy-start.11 = (s32[2]{0:T(128)S(1)}, s32[2]{0:T(128)}, u32[]{:S(2)}) copy-start(s32[2]{0:T(128)} %param.21) | copy-start | bytes 28
  7.2 8.3 %copy-start.10 = (s32[2]{0:T(128)S(1)}, s32[2]{0:T(128)}, u32[]{:S(2)}) copy-start(s32[2]{0:T(128)} %param.22) | copy-start | bytes 28
  7.2 333.1 %all-reduce.4.cloned.1.call-start = ((), (), s32[]{:S(2)}) async-start(), calls=%async_computation | async-start | bytes 524288 | tf_op jit(solution)/shard_map/psum | solution.py:107
  9.5 33.0 %collective-permute-start = (f32[2,2,4,64,128]{4,3,2,1,0:T(8,128)}, f32[2,2,4,64,128]{4,3,2,1,0:T(8,128)S(1)}, u32[]{:S(2)}, u32[]{:S(2)}) collective-permute-start(f32[2,2,4,64,128]{4,3,2,1,0:T(8,128)} %get-tuple-element.20), channel_id=1, source_target_pairs={{16,0},{32,16},{48,32},{64,48},{80,64},{96,80},{112,96},{128,112},... | collective-permute-start | bytes 1572872 | tf_op jit(solution)/shard_map/ppermute | solution.py:18
  10.8 31.7 %collective-permute-start.1 = (f32[2,2,4,64,128]{4,3,2,1,0:T(8,128)}, f32[2,2,4,64,128]{4,3,2,1,0:T(8,128)S(1)}, u32[]{:S(2)}, u32[]{:S(2)}) collective-permute-start(f32[2,2,4,64,128]{4,3,2,1,0:T(8,128)} %get-tuple-element.21), channel_id=1, source_target_pairs={{0,16},{16,32},{32,48},{48,64},{64,80},{80,96},{96,112},{112,128},... | collective-permute-start | bytes 1572872 | tf_op jit(solution)/shard_map/ppermute | solution.py:15
  16.9 24.9 %copy-start.12 = (s32[2]{0:T(128)S(1)}, s32[2]{0:T(128)}, u32[]{:S(2)}) copy-start(s32[2]{0:T(128)} %param.24) | copy-start | bytes 28
  16.9 25.0 %copy-start = (f32[2,8,64,128]{3,2,1,0:T(8,128)S(1)}, f32[2,8,64,128]{3,2,1,0:T(8,128)}, u32[]{:S(2)}) copy-start(f32[2,8,64,128]{3,2,1,0:T(8,128)} %param.14) | copy-start | bytes 1572868
  16.9 25.0 %copy-start.1 = (f32[2,8,64,128]{3,2,1,0:T(8,128)S(1)}, f32[2,8,64,128]{3,2,1,0:T(8,128)}, u32[]{:S(2)}) copy-start(f32[2,8,64,128]{3,2,1,0:T(8,128)} %param.16) | copy-start | bytes 1572868
  41.7 0.7 copy-start.13
  43.0 2.5 copy-start.2
  43.0 2.5 copy-start.4
  43.0 2.5 copy-start.5
  47.0 32.0 %collective-permute-start.2 = (f32[2,2,4,64,128]{4,3,2,1,0:T(8,128)}, f32[2,2,4,64,128]{4,3,2,1,0:T(8,128)}, u32[]{:S(2)}, u32[]{:S(2)}) collective-permute-start(f32[2,2,4,64,128]{4,3,2,1,0:T(8,128)} %get-tuple-element.16), channel_id=1, source_target_pairs={{16,0},{32,16},{48,32},{64,48},{80,64},{96,80},{112,96},{128,112},... | collective-permute-start | bytes 1572872 | tf_op jit(solution)/shard_map/ppermute | solution.py:18
  48.3 30.7 %collective-permute-start.3 = (f32[2,2,4,64,128]{4,3,2,1,0:T(8,128)}, f32[2,2,4,64,128]{4,3,2,1,0:T(8,128)}, u32[]{:S(2)}, u32[]{:S(2)}) collective-permute-start(f32[2,2,4,64,128]{4,3,2,1,0:T(8,128)} %get-tuple-element.17), channel_id=1, source_target_pairs={{0,16},{16,32},{32,48},{48,64},{64,80},{80,96},{96,112},{112,128},... | collective-permute-start | bytes 1572872 | tf_op jit(solution)/shard_map/ppermute | solution.py:15
  80.7 2.5 copy-start.3
Sparse Core Ops, SparseCore 0:
  85.6 254.6 all-reduce.3
where the time goes:
time: 349 us
  waiting for transfers between devices  255 us (73%)
  other arithmetic  64.6 us (19%)
  between operations  14.5 us (4%)
  starting transfers between devices  12 us (3%)
    psum x1, waiting for transfers between devices, per_device(): image = lax.psum(local_sum, 'shots')  255 us
    scatter-add x4, other arithmetic, inject(): jnp.zeros((count, length * plane), jnp.float32).at[rows, flat].add(amounts)  50.8 us
    ppermute x2, starting transfers between devices, extended(): lax.ppermute(lax.slice_in_dim(block, block.shape[dim] - width, None, axis...  9.39 us
  transfers between devices with their start and end apart: 5, of which 1 were waited for; matrix products, arithmetic and copies ran while one was open for 15% of the time, Pallas kernels for 0%

commit v1 on v0

--- a/solution.py
+++ b/solution.py
@@ -104,7 +104,8 @@
     local_sum = terms[0]
     for extra in terms[1:]:
         local_sum = local_sum + extra
-    image = lax.psum(local_sum, "shots")
+    parts = lax.all_gather(local_sum, "shots")
+    image = jnp.sum(parts, axis=0)
     return (src_last, rcv_last, image)
 
 

time: 349 us -> 261 us (0.75)
  waiting for transfers between devices: 255 us -> 164 us
    psum x1 -> x0, waiting for transfers between devices: 255 us -> none  [per_device(): image = lax.psum(local_sum, 'shots')]
    all_gather x0 -> x1, waiting for transfers between devices: none -> 164 us  [per_device(): parts = lax.all_gather(local_sum, 'shots')]
  transfers between devices with their start and end apart: 5 -> 5, of which waited for: 1 -> 1; matrix products, arithmetic and copies ran while one was open for 15% -> 20% of each run, Pallas kernels for 0% -> 0%
where the time goes in v1:
time: 261 us; the launch traced here: 260 us
  waiting for transfers between devices  164 us (63%)
  other arithmetic  67.7 us (26%)
  between operations  14.5 us (6%)
  starting transfers between devices  12 us (5%)
    all_gather x1, waiting for transfers between devices, per_device(): parts = lax.all_gather(local_sum, 'shots')  164 us
    scatter-add x4, other arithmetic, inject(): jnp.zeros((count, length * plane), jnp.float32).at[rows, flat].add(amounts)  50.8 us
    ppermute x2, starting transfers between devices, extended(): lax.ppermute(lax.slice_in_dim(block, block.shape[dim] - width, None, axis...  9.39 us
  transfers between devices with their start and end apart: 5, of which 1 were waited for; matrix products, arithmetic and copies ran while one was open for 20% of the time, Pallas kernels for 0%

profile of v1, /device:TPU:1, one launch (start us, length us, event | category | flops | bytes accessed | tf_op | source)
XLA Modules:
  0.0 259.6 jit_solution(3497826345116781391)
XLA Ops:
  7.2 0.0 copy-start.7
  7.2 0.0 copy-start.6
  7.2 0.0 copy-start.8
  7.2 0.0 copy-start.9
  7.2 0.0 copy-start.11
  7.2 0.0 copy-start.10
  7.2 0.0 all-gather.3.cloned.1.call-start
  7.3 2.3 fusion.58
  9.5 1.3 collective-permute-start
  10.8 4.6 %collective-permute-start.1 = (f32[2,2,4,64,128]{4,3,2,1,0:T(8,128)}, f32[2,2,4,64,128]{4,3,2,1,0:T(8,128)S(1)}, u32[]{:S(2)}, u32[]{:S(2)}) collective-permute-start(f32[2,2,4,64,128]{4,3,2,1,0:T(8,128)} %get-tuple-element.21), channel_id=1, source_target_pairs={{0,16},{16,32},{32,48},{48,64},{64,80},{80,96},{96,112},{112,128},... | collective-permute-start | bytes 1572872 | tf_op jit(solution)/shard_map/ppermute | solution.py:15
  15.5 0.0 copy-done.7
  15.5 0.0 copy-done.6
  15.5 0.0 copy-done.8
  15.5 0.0 copy-done.9
  15.5 0.0 copy-done.11
  15.6 0.0 copy-done.10
  15.6 0.1 copy.18
  15.7 0.2 fusion.83
  15.9 0.1 broadcast.180.clone.1
  16.1 0.6 scatter_fusion
  16.8 0.1 broadcast.180.clone
  16.9 0.0 copy-start.12
  16.9 0.0 copy-start
  16.9 0.0 copy-start.1
  16.9 24.8 %scatter_fusion.1 = f32[2,65536]{1,0:T(2,128)S(1)} fusion(f32[2,65536]{1,0:T(2,128)S(1)} %broadcast.180.clone, s32[512]{0:T(512)S(1)} %bitcast.88, f32[512]{0:T(512)S(1)} %bitcast.113), kind=kCustom, calls=%fused_computation.1 | custom fusion | flops 512 | bytes 10240 | tf_op jit(solution)/shard_map/scatter-add | solution.py:67
  41.7 0.0 copy-start.13
  41.8 0.0 copy-done.12
  41.8 0.1 abs_compare_fusion
  41.9 0.0 copy-done
  41.9 0.0 copy-done.1
  41.9 0.1 pad_maximum_fusion.2
  42.0 0.4 copy-done.13
  42.4 0.1 abs_compare_fusion.1
  42.5 0.1 and_convert_fusion
  42.6 0.0 collective-permute-done
  42.6 0.0 collective-permute-done.1
  42.6 0.4 pad_maximum_fusion
  43.0 0.0 copy-start.2
  43.0 0.0 copy-start.4
  43.0 0.0 copy-start.5
  43.0 2.5 fusion.6
  45.5 0.0 copy-done.2
  45.5 0.0 copy-done.4
  45.5 0.0 copy-done.5
  45.5 0.5 fusion.71
  46.0 1.0 fusion.56
  47.0 1.3 collective-permute-start.2
  48.3 4.8 %collective-permute-start.3 = (f32[2,2,4,64,128]{4,3,2,1,0:T(8,128)}, f32[2,2,4,64,128]{4,3,2,1,0:T(8,128)}, u32[]{:S(2)}, u32[]{:S(2)}) collective-permute-start(f32[2,2,4,64,128]{4,3,2,1,0:T(8,128)} %get-tuple-element.17), channel_id=1, source_target_pairs={{0,16},{16,32},{32,48},{48,64},{64,80},{80,96},{96,112},{112,128},... | collective-permute-start | bytes 1572872 | tf_op jit(solution)/shard_map/ppermute | solution.py:15
  53.1 0.1 broadcast.180.clone.3
  53.3 0.6 scatter_fusion.2
  54.0 0.1 broadcast.180.clone.2
  54.1 24.8 %scatter_fusion.3 = f32[2,65536]{1,0:T(2,128)S(1)} fusion(f32[2,65536]{1,0:T(2,128)S(1)} %broadcast.180.clone.2, s32[512]{0:T(512)S(1)} %bitcast.89, f32[512]{0:T(512)S(1)} %bitcast.112), kind=kCustom, calls=%fused_computation.3 | custom fusion | flops 512 | bytes 10240 | tf_op jit(solution)/shard_map/scatter-add | solution.py:67
  78.9 0.1 pad_maximum_fusion.3
  79.0 0.0 collective-permute-done.2
  79.0 0.0 collective-permute-done.3
  79.0 1.6 pad_maximum_fusion.1
  80.7 0.0 copy-start.3
  80.7 2.5 fusion.26
  83.1 0.0 copy-done.3
  83.1 1.6 multiply_reduce_fusion
  84.8 0.7 add.295
  85.5 0.0 all-gather.3.cloned.1.call-update
  85.5 164.1 %all-gather.3.cloned.1.call-done = f32[128,64,128]{2,1,0:T(8,128)} async-done(((f32[8,64,128]{2,1,0:T(8,128)}), f32[128,64,128]{2,1,0:T(8,128)}) %all-gather.3.cloned.1.call-update) | async-done | bytes 4194320 | tf_op jit(solution)/shard_map/all_gather | solution.py:107
  249.6 3.2 %reduce_sum.29 = f32[8,64,128]{2,1,0:T(8,128)} reduce(f32[16,8,64,128]{3,2,1,0:T(8,128)} %bitcast.106, f32[]{:T(128)} %constant.62.clone.1), dimensions={0}, to_apply=%region_6.7 | reduce | flops 983040 | bytes 4456452 | tf_op jit(solution)/shard_map/reduce_sum | solution.py:108
  (15 shorter events, 0.2 us)
Async XLA Ops:
  7.2 8.3 %copy-start.7 = (f32[2,2,256]{2,1,0:T(2,128)S(1)}, f32[2,2,256]{2,1,0:T(2,128)}, u32[]{:S(2)}) copy-start(f32[2,2,256]{2,1,0:T(2,128)} %param.19) | copy-start | bytes 12292
  7.2 8.3 %copy-start.6 = (s32[2,256]{1,0:T(2,128)S(1)}, s32[2,256]{1,0:T(2,128)}, u32[]{:S(2)}) copy-start(s32[2,256]{1,0:T(2,128)} %param.25) | copy-start | bytes 6148
  7.2 8.3 %copy-start.8 = (f32[2,2]{1,0:T(2,128)S(1)}, f32[2,2]{1,0:T(2,128)}, u32[]{:S(2)}) copy-start(f32[2,2]{1,0:T(2,128)} %param.18) | copy-start | bytes 52
  7.2 8.3 %copy-start.9 = (s32[2]{0:T(128)S(1)}, s32[2]{0:T(128)}, u32[]{:S(2)}) copy-start(s32[2]{0:T(128)} %param.20) | copy-start | bytes 28
  7.2 8.3 %copy-start.11 = (s32[2]{0:T(128)S(1)}, s32[2]{0:T(128)}, u32[]{:S(2)}) copy-start(s32[2]{0:T(128)} %param.21) | copy-start | bytes 28
  7.2 8.3 %copy-start.10 = (s32[2]{0:T(128)S(1)}, s32[2]{0:T(128)}, u32[]{:S(2)}) copy-start(s32[2]{0:T(128)} %param.22) | copy-start | bytes 28
  7.2 242.4 %all-gather.3.cloned.1.call-start = ((), (), s32[]{:S(2)}) async-start(), calls=%async_computation | async-start | bytes 4456448 | tf_op jit(solution)/shard_map/all_gather | solution.py:107
  9.5 33.0 %collective-permute-start = (f32[2,2,4,64,128]{4,3,2,1,0:T(8,128)}, f32[2,2,4,64,128]{4,3,2,1,0:T(8,128)S(1)}, u32[]{:S(2)}, u32[]{:S(2)}) collective-permute-start(f32[2,2,4,64,128]{4,3,2,1,0:T(8,128)} %get-tuple-element.20), channel_id=1, source_target_pairs={{16,0},{32,16},{48,32},{64,48},{80,64},{96,80},{112,96},{128,112},... | collective-permute-start | bytes 1572872 | tf_op jit(solution)/shard_map/ppermute | solution.py:18
  10.8 31.7 %collective-permute-start.1 = (f32[2,2,4,64,128]{4,3,2,1,0:T(8,128)}, f32[2,2,4,64,128]{4,3,2,1,0:T(8,128)S(1)}, u32[]{:S(2)}, u32[]{:S(2)}) collective-permute-start(f32[2,2,4,64,128]{4,3,2,1,0:T(8,128)} %get-tuple-element.21), channel_id=1, source_target_pairs={{0,16},{16,32},{32,48},{48,64},{64,80},{80,96},{96,112},{112,128},... | collective-permute-start | bytes 1572872 | tf_op jit(solution)/shard_map/ppermute | solution.py:15
  16.9 24.9 %copy-start.12 = (s32[2]{0:T(128)S(1)}, s32[2]{0:T(128)}, u32[]{:S(2)}) copy-start(s32[2]{0:T(128)} %param.24) | copy-start | bytes 28
  16.9 25.0 %copy-start = (f32[2,8,64,128]{3,2,1,0:T(8,128)S(1)}, f32[2,8,64,128]{3,2,1,0:T(8,128)}, u32[]{:S(2)}) copy-start(f32[2,8,64,128]{3,2,1,0:T(8,128)} %param.14) | copy-start | bytes 1572868
  16.9 25.0 %copy-start.1 = (f32[2,8,64,128]{3,2,1,0:T(8,128)S(1)}, f32[2,8,64,128]{3,2,1,0:T(8,128)}, u32[]{:S(2)}) copy-start(f32[2,8,64,128]{3,2,1,0:T(8,128)} %param.16) | copy-start | bytes 1572868
  41.7 0.7 copy-start.13
  43.0 2.5 copy-start.2
  43.0 2.5 copy-start.4
  43.0 2.5 copy-start.5
  47.0 32.0 %collective-permute-start.2 = (f32[2,2,4,64,128]{4,3,2,1,0:T(8,128)}, f32[2,2,4,64,128]{4,3,2,1,0:T(8,128)}, u32[]{:S(2)}, u32[]{:S(2)}) collective-permute-start(f32[2,2,4,64,128]{4,3,2,1,0:T(8,128)} %get-tuple-element.16), channel_id=1, source_target_pairs={{16,0},{32,16},{48,32},{64,48},{80,64},{96,80},{112,96},{128,112},... | collective-permute-start | bytes 1572872 | tf_op jit(solution)/shard_map/ppermute | solution.py:18
  48.3 30.7 %collective-permute-start.3 = (f32[2,2,4,64,128]{4,3,2,1,0:T(8,128)}, f32[2,2,4,64,128]{4,3,2,1,0:T(8,128)}, u32[]{:S(2)}, u32[]{:S(2)}) collective-permute-start(f32[2,2,4,64,128]{4,3,2,1,0:T(8,128)} %get-tuple-element.17), channel_id=1, source_target_pairs={{0,16},{16,32},{32,48},{48,64},{64,80},{80,96},{96,112},{112,128},... | collective-permute-start | bytes 1572872 | tf_op jit(solution)/shard_map/ppermute | solution.py:15
  80.7 2.5 copy-start.3
Sparse Core Ops, SparseCore 0:
  85.6 163.9 all-gather.2
